TPU v7x, 256 devices: a whole 4x4x8 slice. The times are simulated.
256 devices in a mesh: leaf: 2 (over core), row: 4 (over x), col: 32 (over z, y).
Axes of the slice: x: 4, y: 4, z: 8, core: 2. Of those that a mesh axis runs over, the one named last changes fastest.
Arguments:
- child_rhs: float32 [512, 256, 256], P(('leaf', 'row', 'col')), may hold values from -6 to 6
- child_diag: float32 [512, 256, 256], P(('leaf', 'row', 'col')), may hold values from -0.375 to 0.375
- child_off: float32 [512, 256, 256], P(('leaf', 'row', 'col')), may hold values from -0.046875 to 0.046875
- live: int32 [512], P(('leaf', 'row', 'col')), may hold values from 1 to 256, 81920 in all
- targets: int32 [512, 256], P(('leaf', 'row', 'col')), may hold values from 0 to 2047
- top_rhs: float32 [2048, 256], P('row'), may hold values from -6 to 6
- top_factor: float32 [2048, 2048], P('row', 'col'), may hold values from -0.125 to 0.125
- top_diag: float32 [2048, 512], P('row'), may hold values from -0.25 to 0.25
Outputs:
- child_sol: float32 [512, 256, 256], P(('leaf', 'row', 'col'))
- top_sol: float32 [2048, 256], P('row')
All inputs are finite; a program needn't handle non-finite values. No bound on the sum of `live` on one device may be relied on, other than what follows from the above.
Results may differ from a plain program's by a relative error of at most 0.0003.
Values sent between devices are 32-bit elements; how exact they have to be, the bound alone decides.
A program may use at most 64 MiB of HBM per device.

v0:
```python
import jax
import jax.numpy as jnp
from jax import lax
from jax.sharding import PartitionSpec as P


def spread(value, axis, source):
    kept = jnp.where(lax.axis_index(axis) == source, value, 0).astype(value.dtype)
    return lax.psum(kept, axis)


def unit_lower(matrix):
    return jnp.tril(matrix) + jnp.eye(matrix.shape[-1], dtype=matrix.dtype)


def shards(child_rhs, child_diag, child_off, live, targets, top_rhs, top_factor, top_diag):
    highest = lax.Precision.HIGHEST
    owned_rows = top_rhs.shape[0]
    right_count = top_rhs.shape[1]
    block_size = top_diag.shape[1]
    owned_blocks = owned_rows // block_size
    row_count = lax.axis_size("row")
    top_order = owned_rows * row_count
    col_width = top_factor.shape[1]
    my_row = lax.axis_index("row")
    my_col = lax.axis_index("col")
    child_sol = jnp.einsum("bij,bjr->bir", unit_lower(child_diag), child_rhs, precision=highest)
    tiles = jnp.einsum("btj,bjr->btr", child_off, child_sol, precision=highest)
    slot_index = jnp.arange(child_off.shape[1], dtype=jnp.int32)
    keep = slot_index[None, :] < live[:, None]
    tiles = jnp.where(keep[:, :, None], tiles, jnp.zeros_like(tiles))
    contrib = jnp.zeros((top_order, right_count), jnp.float32)
    contrib = contrib.at[targets.reshape(-1)].add(tiles.reshape(-1, right_count))
    row_part = lax.psum_scatter(contrib, "row", scatter_dimension=0, tiled=True)
    share = lax.psum_scatter(row_part, ("leaf", "col"), scatter_dimension=0, tiled=True)
    updates = lax.all_gather(share, ("leaf", "col"), axis=0, tiled=True)
    reduced = top_rhs - updates
    inverse_all = unit_lower(top_diag.reshape(owned_blocks, block_size, block_size))
    col_global = my_col * col_width + jnp.arange(col_width, dtype=jnp.int32)

    def step(block, solution):
        local = block % owned_blocks
        owner = block // owned_blocks
        factor_rows = top_factor
        factor_rows = jnp.where(
            (col_global < block * block_size)[None, :], factor_rows, jnp.zeros_like(factor_rows)
        )
        columns = lax.dynamic_slice_in_dim(solution, my_col * col_width, col_width, 0)
        partial_value = jnp.dot(
            factor_rows, columns, precision=highest, preferred_element_type=jnp.float32
        )
        block_inverse = lax.dynamic_index_in_dim(inverse_all, local, 0, keepdims=False)
        before = lax.psum(partial_value, "col")
        solved = jnp.dot(
            block_inverse, reduced - before, precision=highest, preferred_element_type=jnp.float32
        )
        solved = spread(solved, "row", owner)
        return lax.dynamic_update_slice_in_dim(solution, solved, block * block_size, 0)

    solution = lax.fori_loop(
        0, row_count * owned_blocks, step, jnp.zeros((top_order, right_count), jnp.float32)
    )
    top_sol = lax.dynamic_slice_in_dim(solution, my_row * owned_rows, owned_rows, 0)
    return (child_sol, top_sol)


def solution(mesh):
    in_specs = (
        P(("leaf", "row", "col"), None, None),
        P(("leaf", "row", "col"), None, None),
        P(("leaf", "row", "col"), None, None),
        P(("leaf", "row", "col")),
        P(("leaf", "row", "col"), None),
        P("row", None),
        P("row", "col"),
        P("row", None),
    )
    out_specs = (P(("leaf", "row", "col"), None, None), P("row", None))
    return jax.shard_map(shards, mesh=mesh, in_specs=in_specs, out_specs=out_specs, check_vma=False)
```

profile of v0, /device:TPU:8, one launch (start us, length us, event | category | flops | bytes accessed | tf_op | source)
XLA Modules:
  0.0 1160.2 jit_solution(9631845340324377303)
XLA Ops:
  7.2 0.0 reduce-scatter.3.cloned.1.call-start
  7.3 0.8 iota_compare_fusion.4
  8.1 0.7 copy.18
  8.8 1.2 copy.10
  10.0 1.1 fusion.14
  11.1 0.7 convolution_select_fusion.1
  11.8 4.7 scatter_custom_fusion
  16.5 0.0 reduce-scatter.3.cloned.1.call-update
  16.6 0.0 reduce-scatter.5.cloned.1.call-start
  16.6 35.2 %reduce-scatter.3.cloned.1.call-done = f32[512,256]{1,0:T(8,128)} async-done(((f32[2048,256]{1,0:T(8,128)}), f32[512,256]{1,0:T(8,128)}) %reduce-scatter.3.cloned.1.call-update) | async-done | bytes 524304 | tf_op jit(solution)/shard_map/reduce_scatter | solution.py:34
  51.8 0.1 add_bitcast_fusion
  52.0 142.3 %reduce-scatter.5.cloned.1.call-done = f32[8,256]{1,0:T(8,128)} async-done(((f32[512,256]{1,0:T(8,128)}), f32[8,256]{1,0:T(8,128)}) %reduce-scatter.5.cloned.1.call-update) | async-done | bytes 8208 | tf_op jit(solution)/shard_map/reduce_scatter | solution.py:35
  194.3 126.2 %all_gather.3 = f32[512,256]{1,0:T(8,128)S(1)} all-gather(f32[8,256]{1,0:T(8,128)} %reduce-scatter.5.cloned.1.call-done), channel_id=1, replica_groups=mesh['leaf'=2,'row'=4,'col'=32] {'leaf','col'}, dimensions={0}, use_global_device_ids=true | all-gather | bytes 532480 | tf_op jit(solution)/shard_map/all_gather | solution.py:36
  320.5 0.1 sub.17
  320.6 1.5 broadcast.60.clone
  322.0 829.5 %while.16 = (s32[]{:T(128)}, f32[2048,256]{1,0:T(8,128)}, f32[512,64]{0,1:T(8,128)S(1)}, s32[]{:T(128)}, f32[512,256]{1,0:T(8,128)S(1)}, /*index=5*/f32[1,512,51...) while((s32[]{:T(128)}, f32[2048,256]{1,0:T(8,128)}, ...), condition=%wide.region_6.7_spmd.clone, body=%wide.region_3.6_spmd.clone.sunk | while | flops 906526848 | bytes 11731889 | solution.py:60
  322.1 2.3 fusion.35
  324.4 0.0 all-reduce.5.cloned.1.call-start
  324.5 162.3 %all-reduce.3.cloned.1.call-done = f32[512,256]{1,0:T(8,128)} async-done(((f32[512,256]{1,0:T(8,128)}), f32[512,256]{1,0:T(8,128)}) %all-reduce.3.cloned.1.call-update) | async-done | bytes 524304 | tf_op jit(solution)/shard_map/while/body/eval_jaxpr/psum | solution.py:53
  486.8 3.7 fusion.36
  490.5 46.3 %all-reduce.5.cloned.1.call-done = f32[512,256]{0,1:T(8,128)} async-done(((f32[512,256]{0,1:T(8,128)}), f32[512,256]{0,1:T(8,128)}) %all-reduce.5.cloned.1.call-update) | async-done | bytes 524304 | tf_op jit(solution)/shard_map/while/body/eval_jaxpr/psum | solution.py:9
  536.8 1.2 copy.20
  538.0 0.8 constant_dynamic-update-slice_fusion.2
  538.9 2.3 fusion.35
  541.2 0.0 all-reduce.3.cloned.1.call-update
  541.2 0.0 all-reduce.5.cloned.1.call-start
  541.3 149.5 %all-reduce.3.cloned.1.call-done = f32[512,256]{1,0:T(8,128)} async-done(((f32[512,256]{1,0:T(8,128)}), f32[512,256]{1,0:T(8,128)}) %all-reduce.3.cloned.1.call-update) | async-done | bytes 524304 | tf_op jit(solution)/shard_map/while/body/eval_jaxpr/psum | solution.py:53
  690.8 3.7 fusion.36
  694.5 0.0 all-reduce.5.cloned.1.call-update
  694.5 46.3 %all-reduce.5.cloned.1.call-done = f32[512,256]{0,1:T(8,128)} async-done(((f32[512,256]{0,1:T(8,128)}), f32[512,256]{0,1:T(8,128)}) %all-reduce.5.cloned.1.call-update) | async-done | bytes 524304 | tf_op jit(solution)/shard_map/while/body/eval_jaxpr/psum | solution.py:9
  740.8 1.2 copy.20
  742.0 0.8 constant_dynamic-update-slice_fusion.2
  742.9 2.3 fusion.35
  745.2 0.0 all-reduce.5.cloned.1.call-start
  745.3 149.8 %all-reduce.3.cloned.1.call-done = f32[512,256]{1,0:T(8,128)} async-done(((f32[512,256]{1,0:T(8,128)}), f32[512,256]{1,0:T(8,128)}) %all-reduce.3.cloned.1.call-update) | async-done | bytes 524304 | tf_op jit(solution)/shard_map/while/body/eval_jaxpr/psum | solution.py:53
  895.1 3.7 fusion.36
  898.8 46.3 %all-reduce.5.cloned.1.call-done = f32[512,256]{0,1:T(8,128)} async-done(((f32[512,256]{0,1:T(8,128)}), f32[512,256]{0,1:T(8,128)}) %all-reduce.5.cloned.1.call-update) | async-done | bytes 524304 | tf_op jit(solution)/shard_map/while/body/eval_jaxpr/psum | solution.py:9
  945.1 1.2 copy.20
  946.4 0.8 constant_dynamic-update-slice_fusion.2
  947.2 2.3 fusion.35
  949.5 0.0 all-reduce.3.cloned.1.call-update
  949.6 0.0 all-reduce.5.cloned.1.call-start
  949.6 149.8 %all-reduce.3.cloned.1.call-done = f32[512,256]{1,0:T(8,128)} async-done(((f32[512,256]{1,0:T(8,128)}), f32[512,256]{1,0:T(8,128)}) %all-reduce.3.cloned.1.call-update) | async-done | bytes 524304 | tf_op jit(solution)/shard_map/while/body/eval_jaxpr/psum | solution.py:53
  1099.4 3.7 fusion.36
  1103.2 46.3 %all-reduce.5.cloned.1.call-done = f32[512,256]{0,1:T(8,128)} async-done(((f32[512,256]{0,1:T(8,128)}), f32[512,256]{0,1:T(8,128)}) %all-reduce.5.cloned.1.call-update) | async-done | bytes 524304 | tf_op jit(solution)/shard_map/while/body/eval_jaxpr/psum | solution.py:9
  1149.4 1.2 copy.20
  1150.7 0.8 constant_dynamic-update-slice_fusion.2
  1151.5 1.9 constant_dynamic-slice_fusion
  (28 shorter events, 0.2 us)
Async XLA Ops:
  7.2 2.9 copy-start
  7.2 3.9 copy-start.5
  7.2 44.6 %reduce-scatter.3.cloned.1.call-start = ((), (), s32[]{:S(2)}) async-start(), calls=%async_computation.2 | async-start | bytes 2621440 | tf_op jit(solution)/shard_map/reduce_scatter | solution.py:34
  11.1 5.4 copy-start.2
  11.8 40.0 %copy-start.3 = (f32[512,512]{1,0:T(8,128)S(1)}, f32[512,512]{1,0:T(8,128)}, u32[]{:S(2)}) copy-start(f32[512,512]{1,0:T(8,128)} %param.17) | copy-start | bytes 3145732
  16.6 177.7 %reduce-scatter.5.cloned.1.call-start = ((), (), s32[]{:S(2)}) async-start(), calls=%async_computation.3 | async-start | bytes 532480 | tf_op jit(solution)/shard_map/reduce_scatter | solution.py:35
  16.6 303.9 %copy-start.4 = (f32[512,256]{1,0:T(8,128)S(1)}, f32[512,256]{1,0:T(8,128)}, u32[]{:S(2)}) copy-start(f32[512,256]{1,0:T(8,128)} %param.15) | copy-start | bytes 1572868
  52.0 270.1 %copy-start.1 = (f32[512,64]{0,1:T(8,128)S(1)}, f32[512,64]{0,1:T(8,128)}, u32[]{:S(2)}) copy-start(f32[512,64]{0,1:T(8,128)} %param.16) | copy-start | bytes 393220
  322.0 164.7 %all-reduce.3.cloned.1.call-start = ((), (), s32[]{:S(2)}) async-start(), calls=%async_computation.4 | async-start | bytes 1048576 | tf_op jit(solution)/shard_map/while/body/eval_jaxpr/psum | solution.py:53
  324.4 212.4 %all-reduce.5.cloned.1.call-start = ((), (), s32[]{:S(2)}) async-start(), calls=%async_computation.5 | async-start | bytes 1048576 | tf_op jit(solution)/shard_map/while/body/eval_jaxpr/psum | solution.py:9
  538.9 151.9 %all-reduce.3.cloned.1.call-start = ((), (), s32[]{:S(2)}) async-start(), calls=%async_computation.4 | async-start | bytes 1048576 | tf_op jit(solution)/shard_map/while/body/eval_jaxpr/psum | solution.py:53
  541.2 199.6 %all-reduce.5.cloned.1.call-start = ((), (), s32[]{:S(2)}) async-start(), calls=%async_computation.5 | async-start | bytes 1048576 | tf_op jit(solution)/shard_map/while/body/eval_jaxpr/psum | solution.py:9
  742.9 152.2 %all-reduce.3.cloned.1.call-start = ((), (), s32[]{:S(2)}) async-start(), calls=%async_computation.4 | async-start | bytes 1048576 | tf_op jit(solution)/shard_map/while/body/eval_jaxpr/psum | solution.py:53
  745.2 199.9 %all-reduce.5.cloned.1.call-start = ((), (), s32[]{:S(2)}) async-start(), calls=%async_computation.5 | async-start | bytes 1048576 | tf_op jit(solution)/shard_map/while/body/eval_jaxpr/psum | solution.py:9
  947.2 152.2 %all-reduce.3.cloned.1.call-start = ((), (), s32[]{:S(2)}) async-start(), calls=%async_computation.4 | async-start | bytes 1048576 | tf_op jit(solution)/shard_map/while/body/eval_jaxpr/psum | solution.py:53
  949.6 199.9 %all-reduce.5.cloned.1.call-start = ((), (), s32[]{:S(2)}) async-start(), calls=%async_computation.5 | async-start | bytes 1048576 | tf_op jit(solution)/shard_map/while/body/eval_jaxpr/psum | solution.py:9
Sparse Core Ops, SparseCore 0:
  16.7 35.0 reduce-scatter.2
  56.3 137.9 reduce-scatter.4
  327.2 159.4 all-reduce.2
  490.6 46.1 all-reduce.4
  543.7 146.9 all-reduce.2
  694.6 46.1 all-reduce.4
  748.1 146.9 all-reduce.2
  898.9 46.1 all-reduce.4
  952.4 146.9 all-reduce.2
  1103.3 46.1 all-reduce.4
where the time goes:
time: 1160 us
  waiting for transfers between devices  974 us (84%)
  blocking collectives  126 us (11%)
  matrix products  25.9 us (2%)
  between operations  14.2 us (1%)
  local copies, waits for them, and re-layouts  13.6 us (1%)
    psum x4, waiting for transfers between devices, step(): before = lax.psum(partial_value, 'col')  611 us
    psum x4, waiting for transfers between devices, spread(): return lax.psum(kept, axis)  185 us
    reduce_scatter x1, waiting for transfers between devices, shards(): lax.psum_scatter(row_part, ('leaf', 'col'), scatter_dimension=0, tiled=True)  142 us
    all_gather x1, blocking collectives, shards(): updates = lax.all_gather(share, ('leaf', 'col'), axis=0, tiled=True)  126 us
    reduce_scatter x1, waiting for transfers between devices, shards(): row_part = lax.psum_scatter(contrib, 'row', scatter_dimension=0, tiled=True)  35.2 us
  transfers between devices with their start and end apart: 10, of which 10 were waited for; matrix products, arithmetic and copies ran while one was open for 0% of the time, Pallas kernels for 0%

commit v1 on v0

--- a/solution.py
+++ b/solution.py
@@ -33,7 +33,15 @@
     contrib = contrib.at[targets.reshape(-1)].add(tiles.reshape(-1, right_count))
     row_part = lax.psum_scatter(contrib, "row", scatter_dimension=0, tiled=True)
     share = lax.psum_scatter(row_part, ("leaf", "col"), scatter_dimension=0, tiled=True)
-    updates = lax.all_gather(share, ("leaf", "col"), axis=0, tiled=True)
+    updates = jnp.concatenate(
+        lax.all_to_all(
+            jnp.stack([share for _ in range(lax.axis_size(("leaf", "col")))], axis=0),
+            ("leaf", "col"),
+            0,
+            0,
+        ),
+        axis=0,
+    )
     reduced = top_rhs - updates
     inverse_all = unit_lower(top_diag.reshape(owned_blocks, block_size, block_size))
     col_global = my_col * col_width + jnp.arange(col_width, dtype=jnp.int32)

time: 1160 us -> 1050 us (0.905)
  blocking collectives: 126 us -> 0 us
    all_gather x1 -> x0, blocking collectives: 126 us -> none  [shards(): updates = lax.all_gather(share, ('leaf', 'col'), axis=0, tiled=True)]
    psum x4, waiting for transfers between devices: 611 us -> 597 us  [step(): before = lax.psum(partial_value, 'col')]
    all_to_all x0 -> x1, waiting for transfers between devices: none -> 14.4 us  [shards(): lax.all_to_all(jnp.stack([share for _ in range(lax.axis_size(('leaf', 'co...]
  transfers between devices with their start and end apart: 10 -> 11, of which waited for: 10 -> 11; matrix products, arithmetic and copies ran while one was open for 0% -> 0% of each run, Pallas kernels for 0% -> 0%
where the time goes in v1:
time: 1050 us; the launch traced here: 1040 us
  waiting for transfers between devices  974 us (93%)
  matrix products  25.9 us (2%)
  local copies, waits for them, and re-layouts  15.1 us (1%)
  between operations  14.2 us (1%)
    psum x4, waiting for transfers between devices, step(): before = lax.psum(partial_value, 'col')  597 us
    psum x4, waiting for transfers between devices, spread(): return lax.psum(kept, axis)  185 us
    reduce_scatter x1, waiting for transfers between devices, shards(): lax.psum_scatter(row_part, ('leaf', 'col'), scatter_dimension=0, tiled=True)  142 us
    reduce_scatter x1, waiting for transfers between devices, shards(): row_part = lax.psum_scatter(contrib, 'row', scatter_dimension=0, tiled=True)  35.2 us
  transfers between devices with their start and end apart: 11, of which 11 were waited for; matrix products, arithmetic and copies ran while one was open for 0% of the time, Pallas kernels for 0%

profile of v1, /device:TPU:8, one launch (start us, length us, event | category | flops | bytes accessed | tf_op | source)
XLA Modules:
  0.0 1045.0 jit_solution(70767380489810902)
XLA Ops:
  7.2 0.0 reduce-scatter.3.cloned.1.call-start
  7.3 0.8 iota_compare_fusion.4
  8.1 0.7 copy.23
  8.8 1.2 copy.15
  10.0 1.1 fusion.14
  11.1 0.7 convolution_select_fusion.1
  11.8 4.7 scatter_custom_fusion
  16.5 0.0 reduce-scatter.3.cloned.1.call-update
  16.6 0.0 reduce-scatter.5.cloned.1.call-start
  16.6 35.2 %reduce-scatter.3.cloned.1.call-done = f32[512,256]{1,0:T(8,128)} async-done(((f32[2048,256]{1,0:T(8,128)}), f32[512,256]{1,0:T(8,128)}) %reduce-scatter.3.cloned.1.call-update) | async-done | bytes 524304 | tf_op jit(solution)/shard_map/reduce_scatter | solution.py:34
  51.8 0.0 reduce-scatter.5.cloned.1.call-update
  51.8 142.5 %reduce-scatter.5.cloned.1.call-done = f32[8,256]{1,0:T(8,128)} async-done(((f32[512,256]{1,0:T(8,128)}), f32[8,256]{1,0:T(8,128)}) %reduce-scatter.5.cloned.1.call-update) | async-done | bytes 8208 | tf_op jit(solution)/shard_map/reduce_scatter | solution.py:35
  194.3 1.5 stack.2
  195.8 8.4 all-to-all-start
  204.2 1.4 add_bitcast_fusion
  205.6 14.4 %all-to-all-done = f32[64,8,256]{2,1,0:T(8,128)S(1)} async-done(((f32[64,8,256]{2,1,0:T(8,128)}), f32[64,8,256]{2,1,0:T(8,128)S(1)}, u32[]{:S(2)}, u32[]{:S(2)}) %all-to-all-start) | async-done | bytes 524320 | tf_op jit(solution)/shard_map/all_to_all | solution.py:37
  220.0 0.1 bitcast_subtract_fusion
  220.1 1.5 broadcast.62.clone2
  221.6 814.7 %while.16 = (s32[]{:T(128)}, f32[2048,256]{1,0:T(8,128)}, f32[512,64]{0,1:T(8,128)S(1)}, s32[]{:T(128)}, f32[512,256]{1,0:T(8,128)S(1)}, /*index=5*/f32[1,512,51...) while((s32[]{:T(128)}, f32[2048,256]{1,0:T(8,128)}, ...), condition=%wide.region_6.7_spmd.clone, body=%wide.region_3.6_spmd.clone.sunk | while | flops 906526848 | bytes 11731889 | solution.py:68
  221.6 2.3 fusion.35
  224.0 0.0 all-reduce.5.cloned.1.call-start
  224.0 147.5 %all-reduce.3.cloned.1.call-done = f32[512,256]{1,0:T(8,128)} async-done(((f32[512,256]{1,0:T(8,128)}), f32[512,256]{1,0:T(8,128)}) %all-reduce.3.cloned.1.call-update) | async-done | bytes 524304 | tf_op jit(solution)/shard_map/while/body/eval_jaxpr/psum | solution.py:61
  371.5 3.7 fusion.36
  375.2 46.3 %all-reduce.5.cloned.1.call-done = f32[512,256]{0,1:T(8,128)} async-done(((f32[512,256]{0,1:T(8,128)}), f32[512,256]{0,1:T(8,128)}) %all-reduce.5.cloned.1.call-update) | async-done | bytes 524304 | tf_op jit(solution)/shard_map/while/body/eval_jaxpr/psum | solution.py:9
  421.5 1.2 copy.25
  422.7 0.8 constant_dynamic-update-slice_fusion.2
  423.6 2.3 fusion.35
  425.9 0.0 all-reduce.5.cloned.1.call-start
  426.0 149.5 %all-reduce.3.cloned.1.call-done = f32[512,256]{1,0:T(8,128)} async-done(((f32[512,256]{1,0:T(8,128)}), f32[512,256]{1,0:T(8,128)}) %all-reduce.3.cloned.1.call-update) | async-done | bytes 524304 | tf_op jit(solution)/shard_map/while/body/eval_jaxpr/psum | solution.py:61
  575.5 3.7 fusion.36
  579.2 46.3 %all-reduce.5.cloned.1.call-done = f32[512,256]{0,1:T(8,128)} async-done(((f32[512,256]{0,1:T(8,128)}), f32[512,256]{0,1:T(8,128)}) %all-reduce.5.cloned.1.call-update) | async-done | bytes 524304 | tf_op jit(solution)/shard_map/while/body/eval_jaxpr/psum | solution.py:9
  625.5 1.2 copy.25
  626.8 0.8 constant_dynamic-update-slice_fusion.2
  627.6 2.3 fusion.35
  630.0 0.0 all-reduce.5.cloned.1.call-start
  630.0 149.8 %all-reduce.3.cloned.1.call-done = f32[512,256]{1,0:T(8,128)} async-done(((f32[512,256]{1,0:T(8,128)}), f32[512,256]{1,0:T(8,128)}) %all-reduce.3.cloned.1.call-update) | async-done | bytes 524304 | tf_op jit(solution)/shard_map/while/body/eval_jaxpr/psum | solution.py:61
  779.8 3.7 fusion.36
  783.6 46.3 %all-reduce.5.cloned.1.call-done = f32[512,256]{0,1:T(8,128)} async-done(((f32[512,256]{0,1:T(8,128)}), f32[512,256]{0,1:T(8,128)}) %all-reduce.5.cloned.1.call-update) | async-done | bytes 524304 | tf_op jit(solution)/shard_map/while/body/eval_jaxpr/psum | solution.py:9
  829.8 1.2 copy.25
  831.1 0.8 constant_dynamic-update-slice_fusion.2
  831.9 2.3 fusion.35
  834.3 0.0 all-reduce.5.cloned.1.call-start
  834.4 149.8 %all-reduce.3.cloned.1.call-done = f32[512,256]{1,0:T(8,128)} async-done(((f32[512,256]{1,0:T(8,128)}), f32[512,256]{1,0:T(8,128)}) %all-reduce.3.cloned.1.call-update) | async-done | bytes 524304 | tf_op jit(solution)/shard_map/while/body/eval_jaxpr/psum | solution.py:61
  984.1 3.7 fusion.36
  987.9 46.3 %all-reduce.5.cloned.1.call-done = f32[512,256]{0,1:T(8,128)} async-done(((f32[512,256]{0,1:T(8,128)}), f32[512,256]{0,1:T(8,128)}) %all-reduce.5.cloned.1.call-update) | async-done | bytes 524304 | tf_op jit(solution)/shard_map/while/body/eval_jaxpr/psum | solution.py:9
  1034.2 1.2 copy.25
  1035.4 0.8 constant_dynamic-update-slice_fusion.2
  1036.3 1.9 constant_dynamic-slice_fusion
  (28 shorter events, 0.2 us)
Async XLA Ops:
  7.2 2.9 copy-start
  7.2 3.9 copy-start.4
  7.2 44.6 %reduce-scatter.3.cloned.1.call-start = ((), (), s32[]{:S(2)}) async-start(), calls=%async_computation.3 | async-start | bytes 2621440 | tf_op jit(solution)/shard_map/reduce_scatter | solution.py:34
  11.1 5.4 copy-start.2
  16.6 177.7 %reduce-scatter.5.cloned.1.call-start = ((), (), s32[]{:S(2)}) async-start(), calls=%async_computation.4 | async-start | bytes 532480 | tf_op jit(solution)/shard_map/reduce_scatter | solution.py:35
  51.8 168.2 %copy-start.3 = (f32[512,256]{1,0:T(8,128)S(1)}, f32[512,256]{1,0:T(8,128)}, u32[]{:S(2)}) copy-start(f32[512,256]{1,0:T(8,128)} %param.15) | copy-start | bytes 1572868
  195.8 24.2 %all-to-all-start = ((f32[64,8,256]{2,1,0:T(8,128)}), f32[64,8,256]{2,1,0:T(8,128)S(1)}, u32[]{:S(2)}, u32[]{:S(2)}) async-start(f32[64,8,256]{2,1,0:T(8,128)} %stack.2), calls=%async_computation.2 | async-start | bytes 1048576 | tf_op jit(solution)/shard_map/all_to_all | solution.py:37
  205.6 16.0 %copy-start.1 = (f32[512,64]{0,1:T(8,128)S(1)}, f32[512,64]{0,1:T(8,128)}, u32[]{:S(2)}) copy-start(f32[512,64]{0,1:T(8,128)} %param.16) | copy-start | bytes 393220
  221.6 149.9 %all-reduce.3.cloned.1.call-start = ((), (), s32[]{:S(2)}) async-start(), calls=%async_computation.5 | async-start | bytes 1048576 | tf_op jit(solution)/shard_map/while/body/eval_jaxpr/psum | solution.py:61
  224.0 197.5 %all-reduce.5.cloned.1.call-start = ((), (), s32[]{:S(2)}) async-start(), calls=%async_computation.6 | async-start | bytes 1048576 | tf_op jit(solution)/shard_map/while/body/eval_jaxpr/psum | solution.py:9
  423.6 151.9 %all-reduce.3.cloned.1.call-start = ((), (), s32[]{:S(2)}) async-start(), calls=%async_computation.5 | async-start | bytes 1048576 | tf_op jit(solution)/shard_map/while/body/eval_jaxpr/psum | solution.py:61
  425.9 199.6 %all-reduce.5.cloned.1.call-start = ((), (), s32[]{:S(2)}) async-start(), calls=%async_computation.6 | async-start | bytes 1048576 | tf_op jit(solution)/shard_map/while/body/eval_jaxpr/psum | solution.py:9
  627.6 152.2 %all-reduce.3.cloned.1.call-start = ((), (), s32[]{:S(2)}) async-start(), calls=%async_computation.5 | async-start | bytes 1048576 | tf_op jit(solution)/shard_map/while/body/eval_jaxpr/psum | solution.py:61
  630.0 199.9 %all-reduce.5.cloned.1.call-start = ((), (), s32[]{:S(2)}) async-start(), calls=%async_computation.6 | async-start | bytes 1048576 | tf_op jit(solution)/shard_map/while/body/eval_jaxpr/psum | solution.py:9
  831.9 152.2 %all-reduce.3.cloned.1.call-start = ((), (), s32[]{:S(2)}) async-start(), calls=%async_computation.5 | async-start | bytes 1048576 | tf_op jit(solution)/shard_map/while/body/eval_jaxpr/psum | solution.py:61
  834.3 199.9 %all-reduce.5.cloned.1.call-start = ((), (), s32[]{:S(2)}) async-start(), calls=%async_computation.6 | async-start | bytes 1048576 | tf_op jit(solution)/shard_map/while/body/eval_jaxpr/psum | solution.py:9
Sparse Core Ops, SparseCore 0:
  16.7 35.0 reduce-scatter.2
  56.3 137.9 reduce-scatter.4
  226.8 144.6 all-reduce.2
  375.3 46.1 all-reduce.4
  428.5 146.9 all-reduce.2
  579.3 46.1 all-reduce.4
  632.8 146.9 all-reduce.2
  783.7 46.1 all-reduce.4
  837.1 146.9 all-reduce.2
  988.0 46.1 all-reduce.4
